TPU v7x, 128 devices: a whole 4x4x4 slice. The times are simulated.
128 devices in a mesh: grp: 16 (over z, y), tok: 8 (over x, core).
Axes of the slice: x: 4, y: 4, z: 4, core: 2. Of those that a mesh axis runs over, the one named last changes fastest.
Arguments:
- queries: bfloat16 [16384, 5120], P(('grp', 'tok')), may hold values from -6 to 6
- rotated_keys_values: bfloat16 [16384, 2048], P(('grp', 'tok')), may hold values from -6 to 6
- prompt_window_index: int32 [16, 1024], P('grp', 'tok'), may hold values from 0 to 1, never falling along the last dimension, each value on 1 to 768 neighbouring positions
- residual: bfloat16 [16384, 5120], P(('grp', 'tok')), may hold values from -8 to 8
- ffn_gain: float32 [5120], replicated, may hold values from 0.1 to 1.9
- gate_weight: bfloat16 [5120, 8192], P(None, 'grp'), may hold values from -0.078125 to 0.078125
- up_weight: bfloat16 [5120, 8192], P(None, 'grp'), may hold values from -0.078125 to 0.078125
- paged_cache: bfloat16 [2048, 16, 2048], P(('grp', 'tok')), may hold values from -6 to 6
- page_table: int32 [16, 128], P('grp'), may hold values from 0 to 127, each once within a row
Outputs:
- attended: bfloat16 [16384, 5120], P(('grp', 'tok'))
- hidden: bfloat16 [16384, 8192], P(('grp', 'tok'))
- cache_out: bfloat16 [2048, 16, 2048], P(('grp', 'tok'))
All inputs are finite; a program needn't handle non-finite values.
Results may differ from a plain program's by a relative error of at most 0.012.
Values may be sent and summed in bfloat16 or wider, within the bound.
A program may use at most 128 MiB of HBM per device.

v0:
```python
import math

import jax
import jax.numpy as jnp
from jax import lax
from jax.sharding import PartitionSpec as P

QUERY_HEADS = 40
KEY_VALUE_HEADS = 8
HEAD_SIZE = 128
PAGE_TOKENS = 16


MASK_FILLER = -1e30


def on_device(
    queries,
    rotated_keys_values,
    prompt_window_index,
    residual,
    ffn_gain,
    gate_weight,
    up_weight,
    paged_cache,
    page_table,
):
    count_of_rows = queries.shape[0]
    kv_width = rotated_keys_values.shape[1]
    group_split = QUERY_HEADS // KEY_VALUE_HEADS
    slot_count = paged_cache.shape[0]
    tok_index = lax.axis_index("tok")
    first_row = tok_index * count_of_rows
    grouped_rows = queries.reshape(count_of_rows, KEY_VALUE_HEADS, group_split, HEAD_SIZE)
    own_segment = prompt_window_index[0]
    own_place = first_row + jnp.arange(count_of_rows)
    slot_table = page_table[0]
    score_scale = 1.0 / math.sqrt(HEAD_SIZE)
    initial = (
        jnp.full((count_of_rows, KEY_VALUE_HEADS, group_split), MASK_FILLER, jnp.float32),
        jnp.zeros((count_of_rows, KEY_VALUE_HEADS, group_split), jnp.float32),
        jnp.zeros((count_of_rows, KEY_VALUE_HEADS, group_split, HEAD_SIZE), jnp.float32),
        paged_cache,
    )
    key_value_portion = lax.all_gather(rotated_keys_values, "tok", axis=0, tiled=True)
    seg_piece = lax.all_gather(own_segment, "tok", axis=0, tiled=True)
    count_of_keys = key_value_portion.shape[0]
    rows_of_keys = key_value_portion[:, : KEY_VALUE_HEADS * HEAD_SIZE].reshape(
        count_of_keys, KEY_VALUE_HEADS, HEAD_SIZE
    )
    rows_of_values = key_value_portion[:, KEY_VALUE_HEADS * HEAD_SIZE :].reshape(
        count_of_keys, KEY_VALUE_HEADS, HEAD_SIZE
    )
    key_place = jnp.arange(count_of_keys)
    live_mask = (seg_piece[None, :] == own_segment[:, None]) & (
        key_place[None, :] <= own_place[:, None]
    )
    running = (initial[0], initial[1], initial[2])
    run_max, run_sum, partial_value = running
    scores = (
        jnp.einsum("qgrd,kgd->qgrk", grouped_rows, rows_of_keys, preferred_element_type=jnp.float32)
        * score_scale
    )
    scores = jnp.where(live_mask[:, None, None, :], scores, MASK_FILLER)
    new_max = jnp.maximum(run_max, jnp.max(scores, axis=-1))
    weights = jnp.where(live_mask[:, None, None, :], jnp.exp(scores - new_max[..., None]), 0.0)
    run_sum = jnp.sum(weights, axis=-1)
    partial_value = jnp.einsum(
        "qgrk,kgd->qgrd",
        weights.astype(jnp.bfloat16),
        rows_of_values,
        preferred_element_type=jnp.float32,
    )
    running = (new_max, run_sum, partial_value)
    page_count = count_of_keys // PAGE_TOKENS
    targets = (
        lax.dynamic_slice_in_dim(slot_table, jnp.int32(0) // PAGE_TOKENS, page_count)
        - tok_index * slot_count
    )
    onehot = targets[None, :] == jnp.arange(slot_count)[:, None]
    placed = jnp.dot(
        onehot.astype(jnp.bfloat16),
        key_value_portion.reshape(page_count, PAGE_TOKENS * kv_width),
        preferred_element_type=jnp.float32,
    )
    placed = placed.astype(jnp.bfloat16).reshape(slot_count, PAGE_TOKENS, kv_width)
    written = jnp.where(jnp.any(onehot, axis=1)[:, None, None], placed, initial[3])
    run_sum = running[1]
    partial_value = running[2]
    attention = (
        (partial_value / run_sum[..., None])
        .reshape(count_of_rows, QUERY_HEADS * HEAD_SIZE)
        .astype(jnp.bfloat16)
    )
    attended = (residual.astype(jnp.float32) + attention.astype(jnp.float32)).astype(jnp.bfloat16)
    widened = attended.astype(jnp.float32)
    normed = (
        widened * lax.rsqrt(jnp.mean(widened * widened, axis=-1, keepdims=True) + 1e-06) * ffn_gain
    ).astype(jnp.bfloat16)
    tok_count = lax.axis_size("tok")
    grp_count = lax.axis_size("grp")
    col_width = gate_weight.shape[1] // tok_count
    gate_cols = lax.dynamic_slice_in_dim(gate_weight, tok_index * col_width, col_width, 1)
    up_cols = lax.dynamic_slice_in_dim(up_weight, tok_index * col_width, col_width, 1)
    gate_all, up_all = (
        lax.all_gather(gate_cols, "grp", axis=1, tiled=True),
        lax.all_gather(up_cols, "grp", axis=1, tiled=True),
    )
    shards = lax.all_gather(normed, "tok", axis=0, tiled=True)
    gate_sum = jnp.dot(shards, gate_all, preferred_element_type=jnp.float32)
    up_sum = jnp.dot(shards, up_all, preferred_element_type=jnp.float32)
    produced = (jax.nn.silu(gate_sum) * up_sum).astype(jnp.bfloat16)
    returned = lax.all_to_all(produced, "tok", split_axis=0, concat_axis=1, tiled=True)
    hidden = (
        returned.reshape(count_of_rows, tok_count, grp_count, col_width)
        .transpose(0, 2, 1, 3)
        .reshape(count_of_rows, tok_count * grp_count * col_width)
    )
    return (attended, hidden, written)


def solution(mesh):
    in_specs = (
        P(("grp", "tok"), None),
        P(("grp", "tok"), None),
        P("grp", "tok"),
        P(("grp", "tok"), None),
        P(),
        P(None, "grp"),
        P(None, "grp"),
        P(("grp", "tok"), None, None),
        P("grp", None),
    )
    out_specs = (P(("grp", "tok"), None), P(("grp", "tok"), None), P(("grp", "tok"), None, None))
    return jax.shard_map(
        on_device, mesh=mesh, in_specs=in_specs, out_specs=out_specs, check_vma=False
    )
```

profile of v0, /device:TPU:25, one launch (start us, length us, event | category | flops | bytes accessed | tf_op | source)
XLA Modules:
  0.0 339.1 jit_solution(3943348926296142948)
XLA Ops:
  7.2 2.1 copy.48
  9.4 1.7 constant_dynamic-slice_fusion.1
  11.2 1.3 copy.66
  12.6 1.4 copy.49
  14.0 10.9 %all-gather = s32[1,1024]{1,0:T(1,128)S(1)} all-gather(s32[1,128]{1,0:T(1,128)S(1)} %copy-done.6), channel_id=2, replica_groups=mesh['grp'=16,'tok'=8] {'tok'}, dimensions={1}, use_global_device_ids=true | all-gather | bytes 4608 | tf_op jit(solution)/shard_map/all_gather | solution.py:46
  25.2 23.7 %all-gather.6.cloned.1.call-done = bf16[1024,2048]{0,1:T(8,128)(2,1)} async-done(((bf16[128,2048]{0,1:T(8,128)(2,1)}), bf16[1024,2048]{0,1:T(8,128)(2,1)}) %all-gather.6.cloned.1.call-update) | async-done | bytes 4194320 | tf_op jit(solution)/shard_map/all_gather | solution.py:45
  48.8 4.0 %fusion.18 = (bf16[1024,1024]{0,1:T(8,128)(2,1)S(1)}, bf16[1024,1024]{0,1:T(8,128)(2,1)}) fusion(bf16[1024,2048]{0,1:T(8,128)(2,1)} %all-gather.6.cloned.1.call-done), kind=kLoop, calls=%fused_computation.33 | loop fusion | bytes 8388608 | tf_op jit(solution)/shard_map/slice | solution.py:48
  52.8 4.6 %fusion = (f32[128,8,5]{0,2,1:T(8,128)S(1)}, f32[8,1024,128,5]{2,1,3,0:T(8,128)S(1)}) fusion(pred[128,1024]{0,1:T(8,128)(4,1)S(1)} %fusion.12, bf16[1024,8,128,1]{0,2,3,1:T(8,128)(2,1)S(1)} %bitcast.53, bf16[128,8,5,128]{0,3,2,1:T(8,128)(2,1)} %bitcast.56), kind=kOutput, calls=%fused_computation.3 | convolution fusion | flops 1357900800 | bytes 24530944 | tf_op jit(solution)/shard_map/qgrd,kgd->qgrk/dot_general | solution.py:61
  57.5 5.0 %fusion.1 = f32[128,8,5]{0,2,1:T(8,128)S(1)} fusion(f32[8,1024,128,5]{2,1,3,0:T(8,128)S(1)} %get-tuple-element.20, f32[128,8,5]{0,2,1:T(8,128)S(1)} %broadcast_maximum_fusion, pred[128,1024]{0,1:T(8,128)(4,1)S(1)} %fusion.12), kind=kLoop, calls=%fused_computation.4 | loop fusion | flops 26209280 | bytes 21143552 | tf_op jit(solution)/shard_map/reduce_sum | solution.py:67
  62.5 3.3 copy-done
  65.9 10.3 %fusion.9 = bf16[128,8,5,128]{0,3,2,1:T(8,128)(2,1)S(1)} fusion(bf16[1024,8,128,1]{0,2,3,1:T(8,128)(2,1)S(1)} %bitcast.59, f32[8,1024,128,5]{2,1,3,0:T(8,128)} %copy-done, f32[128,8,5]{0,2,1:T(8,128)S(1)} %broadcast_maximum_fusion, pred[128,1024]{0,1:T(8,128)(4,1)S(1)} %fusion.12, f32[128,8,5]{0,2,1:T(8,128)S(1)} %fusion.1), kind=kOutput, calls=%fused_computation.15 | convolution fusion | flops 1369702400 | bytes 24551424 | tf_op jit(solution)/shard_map/qgrk,kgd->qgrd/dot_general | solution.py:68
  76.2 1.8 bitcast_convert_fusion
  77.9 2.2 copy.53
  80.1 1.8 fusion.6
  81.9 1.0 copy-done.1
  83.0 1.4 fusion.8
  84.7 1.8 constant_dynamic-slice_fusion
  86.4 1.3 copy.67
  87.8 44.9 %all-gather.10.cloned.1.call-done = bf16[5120,1024]{0,1:T(8,128)(2,1)} async-done(((bf16[5120,64]{0,1:T(8,128)(2,1)}), bf16[5120,1024]{0,1:T(8,128)(2,1)}) %all-gather.10.cloned.1.call-update) | async-done | bytes 10485776 | tf_op jit(solution)/shard_map/all_gather | solution.py:106
  132.7 60.8 %all-gather.8.cloned.1.call-done = bf16[1024,5120]{1,0:T(8,128)(2,1)} async-done(((bf16[128,5120]{1,0:T(8,128)(2,1)}), bf16[1024,5120]{1,0:T(8,128)(2,1)}) %all-gather.8.cloned.1.call-update) | async-done | bytes 10485776 | tf_op jit(solution)/shard_map/all_gather | solution.py:109
  193.5 17.3 %fusion.19 = f32[1024,1024]{1,0:T(8,128)} fusion(bf16[1024,5120]{1,0:T(8,128)(2,1)} %all-gather.8.cloned.1.call-done, bf16[5120,1024]{0,1:T(8,128)(2,1)} %all-gather.10.cloned.1.call-done), kind=kOutput, calls=%fused_computation.34 | convolution fusion | flops 10737418240 | bytes 25165824 | tf_op jit(solution)/shard_map/dot_general | solution.py:110
  210.8 65.1 %all-gather.12.cloned.1.call-done = bf16[5120,1024]{0,1:T(8,128)(2,1)} async-done(((bf16[5120,64]{0,1:T(8,128)(2,1)}), bf16[5120,1024]{0,1:T(8,128)(2,1)}) %all-gather.12.cloned.1.call-update) | async-done | bytes 10485776 | tf_op jit(solution)/shard_map/all_gather | solution.py:107
  275.9 17.3 %multiply_convert_fusion = bf16[1024,1024]{1,0:T(8,128)(2,1)S(1)} fusion(f32[1024,1024]{1,0:T(8,128)} %fusion.19, bf16[1024,5120]{1,0:T(8,128)(2,1)} %all-gather.8.cloned.1.call-done, bf16[5120,1024]{0,1:T(8,128)(2,1)} %all-gather.12.cloned.1.call-done), kind=kOutput, calls=%fused_computation.8 | convolution fusion | flops 10743709696 | bytes 27262976 | tf_op jit(solution)/shard_map/dot_general | solution.py:111
  293.2 2.4 copy.56
  295.6 5.0 %all-to-all-start = ((bf16[8,128,1024]{1,2,0:T(8,128)(2,1)}), bf16[8,128,1024]{1,2,0:T(8,128)(2,1)S(1)}, u32[]{:S(2)}, u32[]{:S(2)}) async-start(bf16[8,128,1024]{1,2,0:T(8,128)(2,1)} %copy.56), calls=%async_computation | async-start | bytes 4194304 | tf_op jit(solution)/shard_map/all_to_all | solution.py:113
  300.7 6.5 %copy.58 = bf16[1024,2048]{1,0:T(8,128)(2,1)} copy(bf16[1024,2048]{0,1:T(8,128)(2,1)} %all-gather.6.cloned.1.call-done) | data formatting | bytes 8388608 | tf_op jit(solution)/shard_map/all_gather | solution.py:45
  307.2 7.5 %reshape.103 = bf16[64,32768]{1,0:T(8,128)(2,1)} reshape(bf16[1024,2048]{1,0:T(8,128)(2,1)} %copy.58) | data formatting | bytes 8388608 | tf_op jit(solution)/shard_map/reshape | solution.py:83
  314.6 2.9 convolution_convert_fusion
  318.2 1.1 bitcast_select_fusion.1
  319.3 7.6 %all-to-all-done = bf16[8,128,1024]{1,2,0:T(8,128)(2,1)S(1)} async-done(((bf16[8,128,1024]{1,2,0:T(8,128)(2,1)}), bf16[8,128,1024]{1,2,0:T(8,128)(2,1)S(1)}, u32[]{:S(2)}, u32[]{:S(2)}) %all-to-all-start) | async-done | bytes 2097184 | tf_op jit(solution)/shard_map/all_to_all | solution.py:113
  326.9 1.6 copy.57
  328.5 4.1 %copy.59 = bf16[128,8192]{1,0:T(8,128)(2,1)} copy(bf16[128,8192]{0,1:T(8,128)(2,1)} %bitcast.55) | data formatting | bytes 4194304
  (29 shorter events, 1.4 us)
Async XLA Ops:
  7.2 5.4 %copy-start.3 = (bf16[128,5120]{1,0:T(8,128)(2,1)S(1)}, bf16[128,5120]{1,0:T(8,128)(2,1)}, u32[]{:S(2)}) copy-start(bf16[128,5120]{1,0:T(8,128)(2,1)} %param.9) | copy-start | bytes 3932164
  7.2 41.7 %all-gather.6.cloned.1.call-start = ((), (), s32[]{:S(2)}) async-start(), calls=%async_computation.1 | async-start | bytes 4718592 | tf_op jit(solution)/shard_map/all_gather | solution.py:45
  9.4 4.7 %copy-start.6 = (s32[1,128]{1,0:T(1,128)S(1)}, s32[1,128]{1,0:T(1,128)}, u32[]{:S(2)}) copy-start(s32[1,128]{1,0:T(1,128)} %param.11) | copy-start | bytes 1540
  9.4 123.3 %all-gather.10.cloned.1.call-start = ((), (), s32[]{:S(2)}) async-start(), calls=%async_computation.3 | async-start | bytes 11141120 | tf_op jit(solution)/shard_map/all_gather | solution.py:106
  12.5 181.0 %all-gather.8.cloned.1.call-start = ((), (), s32[]{:S(2)}) async-start(), calls=%async_computation.2 | async-start | bytes 11796480 | tf_op jit(solution)/shard_map/all_gather | solution.py:109
  57.5 8.4 %copy-start = (f32[8,1024,128,5]{2,1,3,0:T(8,128)}, f32[8,1024,128,5]{2,1,3,0:T(8,128)S(1)}, u32[]{:S(2)}) copy-start(f32[8,1024,128,5]{2,1,3,0:T(8,128)S(1)} %get-tuple-element.20) | copy-start | bytes 62914564
  57.5 8.4 %copy-start.2 = (bf16[1024,1024]{0,1:T(8,128)(2,1)S(1)}, bf16[1024,1024]{0,1:T(8,128)(2,1)}, u32[]{:S(2)}) copy-start(bf16[1024,1024]{0,1:T(8,128)(2,1)} %get-tuple-element.18) | copy-start | bytes 6291460
  77.9 5.0 %copy-start.5 = (f32[5120]{0:T(1024)S(1)}, f32[5120]{0:T(1024)}, u32[]{:S(2)}) copy-start(f32[5120]{0:T(1024)} %param.13) | copy-start | bytes 61444
  81.9 1.1 copy-start.1
  84.4 191.5 %all-gather.12.cloned.1.call-start = ((), (), s32[]{:S(2)}) async-start(), calls=%async_computation.4 | async-start | bytes 11141120 | tf_op jit(solution)/shard_map/all_gather | solution.py:107
  293.2 7.4 %copy-start.7 = (s32[1,128]{1,0:T(1,128)S(1)}, s32[1,128]{1,0:T(1,128)}, u32[]{:S(2)}) copy-start(s32[1,128]{1,0:T(1,128)} %param.17) | copy-start | bytes 1540
  295.6 31.3 %all-to-all-start = ((bf16[8,128,1024]{1,2,0:T(8,128)(2,1)}), bf16[8,128,1024]{1,2,0:T(8,128)(2,1)S(1)}, u32[]{:S(2)}, u32[]{:S(2)}) async-start(bf16[8,128,1024]{1,2,0:T(8,128)(2,1)} %copy.56), calls=%async_computation | async-start | bytes 4194304 | tf_op jit(solution)/shard_map/all_to_all | solution.py:113
  314.6 3.5 %copy-start.4 = (bf16[16,16,2048]{2,1,0:T(8,128)(2,1)S(1)}, bf16[16,16,2048]{2,1,0:T(8,128)(2,1)}, u32[]{:S(2)}) copy-start(bf16[16,16,2048]{2,1,0:T(8,128)(2,1)} %param.16) | copy-start | bytes 3145732
Sparse Core Ops, SparseCore 0:
  10.3 38.5 all-gather.5
  51.6 81.0 all-gather.9
  134.9 58.5 all-gather.7
  195.5 80.3 all-gather.11
where the time goes:
time: 341 us; the launch traced here: 339 us
  waiting for transfers between devices  202 us (59%)
  matrix products  52.4 us (15%)
  local copies, waits for them, and re-layouts  42.8 us (13%)
  between operations  13.9 us (4%)
  other arithmetic  11.5 us (3%)
  blocking collectives  10.9 us (3%)
  starting transfers between devices  5.31 us (2%)
    all_gather x1, waiting for transfers between devices, on_device(): lax.all_gather(up_cols, 'grp', axis=1, tiled=True)  65.1 us
    all_gather x1, waiting for transfers between devices, on_device(): shards = lax.all_gather(normed, 'tok', axis=0, tiled=True)  60.8 us
    all_gather x1, waiting for transfers between devices, on_device(): lax.all_gather(gate_cols, 'grp', axis=1, tiled=True)  44.9 us
    all_gather x1, waiting for transfers between devices, on_device(): lax.all_gather(rotated_keys_values, 'tok', axis=0, tiled=True)  23.7 us
    dot_general x1, matrix products, on_device(): up_sum = jnp.dot(shards, up_all, preferred_element_type=jnp.float32)  17.3 us
    dot_general x1, matrix products, on_device(): gate_sum = jnp.dot(shards, gate_all, preferred_element_type=jnp.float32)  17.3 us
    unnamed x22, local copies, waits for them, and re-layouts  15.2 us
    all_gather x1, blocking collectives, on_device(): seg_piece = lax.all_gather(own_segment, 'tok', axis=0, tiled=True)  10.9 us
  transfers between devices with their start and end apart: 5, of which 5 were waited for; matrix products, arithmetic and copies ran while one was open for 22% of the time, Pallas kernels for 0%

commit v1 on v0

v1 whole, which is shorter than its diff:
```python
import math

import jax
import jax.numpy as jnp
from jax import lax
from jax.experimental import pallas as pl
from jax.experimental.pallas import tpu as pltpu
from jax.sharding import PartitionSpec as P

HEADS = 40
KV_HEADS = 8
HEAD = 128
GROUP = HEADS // KV_HEADS
PAGE = 16
WIDTH = HEADS * HEAD
COLS = 128
SIDE = 4
N_TOK = 8
MASKED = -1e30
MESH = pl.DeviceIdType.MESH


def kernel(
    q_in,
    kv_in,
    seg_in,
    res_in,
    gain_in,
    gate_in,
    up_in,
    cache_in,
    table_in,
    att_out,
    hid_out,
    cache_out,
    qbuf,
    kvbuf,
    segbuf,
    resbuf,
    cachebuf,
    placedbuf,
    attbuf,
    biasbuf,
    normbuf,
    wbuf,
    hidbuf,
    kv_send,
    kv_recv,
    nrm_send,
    nrm_recv,
    w_send,
    w_recv,
    seg_send,
    seg_recv,
    hid_send,
    hid_recv,
    local_sem,
):
    rows = q_in.shape[0]
    half = rows // 2
    keys = N_TOK * rows
    slots_here = cache_in.shape[0]
    units = gate_in.shape[1]
    g = lax.axis_index("grp")
    t = lax.axis_index("tok")
    x, c = t // 2, t % 2
    z, y = g // SIDE, g % SIDE
    first = c == 0
    p = jnp.where(first, z, y)
    q = jnp.where(first, y, z)
    p_step = jnp.where(first, SIDE, 1)
    q_step = jnp.where(first, 1, SIDE)

    def wrap(v):
        return (v + SIDE) % SIDE

    def grp_of(pp, qq):
        return pp * p_step + qq * q_step

    x_next = (g, wrap(x + 1) * 2 + c)
    x_prev = (g, wrap(x - 1) * 2 + c)
    sibling = (g, x * 2 + 1 - c)
    p_next = (grp_of(wrap(p + 1), q), t)
    p_prev = (grp_of(wrap(p - 1), q), t)
    q_next = (grp_of(p, wrap(q + 1)), t)
    q_prev = (grp_of(p, wrap(q - 1)), t)
    plane = (p_next, p_prev, q_next, q_prev)
    P_NEXT, P_PREV, Q_NEXT, Q_PREV = 0, 1, 2, 3

    barrier = pltpu.get_barrier_semaphore()
    for there in plane:
        pl.semaphore_signal(barrier, inc=1, device_id=there, device_id_type=MESH)
    for d in range(1, N_TOK):
        pl.semaphore_signal(
            barrier, inc=1, device_id=(g, (t + d) % N_TOK), device_id_type=MESH
        )
    pl.semaphore_wait(barrier, N_TOK + 3)

    source = (p + q) % 2 == c
    x_col = pl.multiple_of(x * COLS, COLS)
    own_slot = q * 2 + p // 2
    far_slot = q * 2 + 1 - p // 2
    prev_slot = q * 2 + wrap(p - 1) // 2
    next_slot = q * 2 + wrap(p + 1) // 2

    def piece(slot, m):
        return wbuf.at[slot, :, pl.ds(m * COLS, COLS)]

    def own_piece(m):
        return (gate_in, up_in)[m].at[:, pl.ds(x_col, COLS)]

    def w_copy(slot, m, way, src=None):
        return pltpu.make_async_remote_copy(
            src_ref=piece(slot, m) if src is None else src,
            dst_ref=piece(slot, m),
            send_sem=w_send.at[way, slot * 2 + m],
            recv_sem=w_recv.at[slot * 2 + m],
            device_id=plane[way],
            device_id_type=MESH,
        )

    def w_wait(slot, m):
        w_copy(slot, m, 0).wait_recv()

    @pl.when(source)
    def _():
        for m in range(2):
            for way in range(4):
                w_copy(own_slot, m, way, own_piece(m)).start()

    def ring(buf, send, recv):
        def copy(slot, n_send, n_recv, there, part=None, src=None):
            ref = buf.at[slot]
            if part is not None:
                ref = ref.at[pl.ds(part * half, half)]
            return pltpu.make_async_remote_copy(
                src_ref=ref if src is None else src,
                dst_ref=ref,
                send_sem=send.at[n_send],
                recv_sem=recv.at[n_recv],
                device_id=there,
                device_id_type=MESH,
            )

        prev_s = wrap(x - 1) * 2 + c
        next_s = wrap(x + 1) * 2 + c
        far_s = wrap(x + 2) * 2 + c
        other = 1 - 2 * c

        def begin(src=None):
            copy(t, 0, 0, x_next, src=src).start()
            copy(t, 1, 1, x_prev, src=src).start()
            copy(t, 2, 4, sibling, src=src).start()

        def relay_near():
            copy(prev_s, 0, 0, x_next).wait_recv()
            copy(prev_s, 3, 2, x_next, part=0).start()
            copy(prev_s, 4, 5, sibling).start()
            copy(next_s, 1, 1, x_prev).wait_recv()
            copy(next_s, 5, 3, x_prev, part=1).start()
            copy(next_s, 6, 6, sibling).start()

        def relay_far():
            copy(far_s, 3, 2, x_next, part=0).wait_recv()
            copy(far_s, 7, 7, sibling, part=0).start()
            copy(far_s, 5, 3, x_prev, part=1).wait_recv()
            copy(far_s, 8, 8, sibling, part=1).start()

        def sibling_own():
            copy(t + other, 2, 4, sibling).wait_recv()

        def sibling_near():
            copy(prev_s + other, 4, 5, sibling).wait_recv()
            copy(next_s + other, 6, 6, sibling).wait_recv()

        def sibling_far():
            copy(far_s + other, 7, 7, sibling, part=0).wait_recv()
            copy(far_s + other, 8, 8, sibling, part=1).wait_recv()

        def drain():
            copy(t, 0, 0, x_next).wait_send()
            copy(t, 1, 1, x_prev).wait_send()
            copy(t, 2, 4, sibling).wait_send()
            copy(prev_s, 3, 2, x_next, part=0).wait_send()
            copy(prev_s, 4, 5, sibling).wait_send()
            copy(next_s, 5, 3, x_prev, part=1).wait_send()
            copy(next_s, 6, 6, sibling).wait_send()
            copy(far_s, 7, 7, sibling, part=0).wait_send()
            copy(far_s, 8, 8, sibling, part=1).wait_send()

        return (
            begin,
            relay_near,
            relay_far,
            sibling_own,
            sibling_near,
            sibling_far,
            drain,
        )

    kv_ring = ring(kvbuf, kv_send, kv_recv)
    kv_ring[0](kv_in)

    def seg_copy(d):
        return pltpu.make_async_remote_copy(
            src_ref=seg_in,
            dst_ref=segbuf.at[t],
            send_sem=seg_send,
            recv_sem=seg_recv,
            device_id=(g, (t + d) % N_TOK),
            device_id_type=MESH,
        )

    for d in range(1, N_TOK):
        seg_copy(d).start()

    load_kv = pltpu.make_async_copy(kv_in, kvbuf.at[t], local_sem.at[0])
    load_q = pltpu.make_async_copy(q_in, qbuf, local_sem.at[1])
    load_res = pltpu.make_async_copy(res_in, resbuf, local_sem.at[2])
    load_cache = pltpu.make_async_copy(cache_in, cachebuf, local_sem.at[3])
    load_seg = pltpu.make_async_copy(seg_in, segbuf.at[t], local_sem.at[4])
    load_gate = pltpu.make_async_copy(own_piece(0), piece(own_slot, 0), local_sem.at[5])
    load_up = pltpu.make_async_copy(own_piece(1), piece(own_slot, 1), local_sem.at[6])
    load_kv.start()
    load_q.start()
    load_seg.start()
    load_res.start()
    load_cache.start()

    @pl.when(source)
    def _():
        load_gate.start()
        load_up.start()

    load_seg.wait()
    pltpu.make_async_copy(segbuf.at[pl.ds(0, N_TOK - 1)], segbuf.at[pl.ds(0, N_TOK - 1)], seg_recv).wait()
    own_seg = jnp.broadcast_to(seg_in[...], (rows, rows)).T
    row_id = lax.broadcasted_iota(jnp.int32, (rows, rows), 0) + t * rows
    col_id = lax.broadcasted_iota(jnp.int32, (rows, rows), 1)
    for i in range(N_TOK):
        live = (own_seg == segbuf[i]) & (col_id + i * rows <= row_id)
        biasbuf[:, i * rows : (i + 1) * rows] = jnp.where(live, 0.0, MASKED)

    kv_ring[1]()

    @pl.when(jnp.logical_not(source))
    def _():
        w_wait(prev_slot, 0)
        w_copy(prev_slot, 0, P_NEXT).start()
        w_copy(prev_slot, 0, Q_NEXT).start()
        w_copy(prev_slot, 0, Q_PREV).start()
        w_wait(next_slot, 0)
        w_copy(next_slot, 0, Q_NEXT).start()
        w_copy(next_slot, 0, Q_PREV).start()

    kv_ring[2]()
    load_kv.wait()
    load_q.wait()
    load_res.wait()
    kv_ring[3]()
    kv_ring[4]()
    kv_ring[5]()

    scale = 1.0 / math.sqrt(HEAD)

    def attend(h, squares):
        base = pl.multiple_of(h * (GROUP * HEAD), HEAD)
        queries = jnp.concatenate(
            [qbuf[:, pl.ds(base + j * HEAD, HEAD)] for j in range(GROUP)], axis=0
        )
        k_col = pl.multiple_of(h * HEAD, HEAD)
        k = kvbuf[:, :, pl.ds(k_col, HEAD)].reshape(keys, HEAD)
        v = kvbuf[:, :, pl.ds(k_col + KV_HEADS * HEAD, HEAD)].reshape(keys, HEAD)
        scores = lax.dot_general(
            queries, k, (((1,), (1,)), ((), ())), preferred_element_type=jnp.float32
        )
        scores = scores.reshape(GROUP, rows, keys) + biasbuf[...][None]
        top = jnp.max(scores, axis=-1, keepdims=True)
        weights = jnp.exp((scores - top) * scale)
        total = jnp.sum(weights, axis=-1, keepdims=True)
        weights = weights.astype(jnp.bfloat16).reshape(GROUP * rows, keys)
        out = jnp.dot(weights, v, preferred_element_type=jnp.float32)
        out = (out.reshape(GROUP, rows, HEAD) / total).astype(jnp.bfloat16)
        for j in range(GROUP):
            cols = pl.ds(base + j * HEAD, HEAD)
            a = resbuf[:, cols].astype(jnp.float32) + out[j].astype(jnp.float32)
            a = a.astype(jnp.bfloat16)
            attbuf[:, cols] = a
            a = a.astype(jnp.float32)
            squares = squares + a * a
        return squares

    squares = lax.fori_loop(
        0, KV_HEADS // 2, attend, jnp.zeros((rows, HEAD), jnp.float32)
    )

    @pl.when(jnp.logical_not(source))
    def _():
        w_wait(prev_slot, 1)
        w_copy(prev_slot, 1, Q_NEXT).start()
        w_copy(prev_slot, 1, Q_PREV).start()
        w_wait(next_slot, 1)
        w_copy(next_slot, 1, P_PREV).start()
        w_copy(next_slot, 1, Q_NEXT).start()
        w_copy(next_slot, 1, Q_PREV).start()

    @pl.when(source)
    def _():
        load_gate.wait()
        load_up.wait()
        w_wait(far_slot, 0)
        w_copy(far_slot, 0, Q_NEXT).start()
        w_copy(far_slot, 0, Q_PREV).start()

    squares = lax.fori_loop(KV_HEADS // 2, KV_HEADS, attend, squares)
    mean = jnp.sum(squares, axis=-1, keepdims=True) * (1.0 / WIDTH)
    inverse = lax.rsqrt(mean + 1e-6)

    def norm(h, carry):
        cols = pl.ds(pl.multiple_of(h * (GROUP * HEAD), HEAD), GROUP * HEAD)
        a = attbuf[:, cols].astype(jnp.float32) * inverse * gain_in[:, cols]
        normbuf[t, :, cols] = a.astype(jnp.bfloat16)
        return carry

    lax.fori_loop(0, KV_HEADS, norm, 0)

    nrm_ring = ring(normbuf, nrm_send, nrm_recv)
    nrm_ring[0]()
    store_att = pltpu.make_async_copy(attbuf, att_out, local_sem.at[7])
    store_att.start()

    @pl.when(source)
    def _():
        w_wait(far_slot, 1)
        w_copy(far_slot, 1, Q_NEXT).start()
        w_copy(far_slot, 1, Q_PREV).start()

    prev_row = wrap(q - 1) * 2
    next_row = wrap(q + 1) * 2
    lead = p // 2

    load_cache.wait()
    table = jnp.broadcast_to(table_in[...], (8, table_in.shape[1]))
    page_id = lax.broadcasted_iota(jnp.int32, (table_in.shape[1], keys), 0)
    key_id = lax.broadcasted_iota(jnp.int32, (table_in.shape[1], keys), 1)
    spread = (page_id == key_id // PAGE).astype(jnp.float32).astype(jnp.bfloat16)
    slot_of = jnp.dot(
        table.astype(jnp.float32).astype(jnp.bfloat16),
        spread,
        preferred_element_type=jnp.float32,
    )
    key_row = lax.broadcasted_iota(jnp.int32, (8, keys), 1)
    key_row = (key_row % PAGE).astype(jnp.float32)
    shift = (t * slots_here).astype(jnp.float32)
    goal = ((slot_of - shift) * PAGE + key_row)[:1]
    here = lax.broadcasted_iota(jnp.int32, (slots_here * PAGE, keys), 0)
    picked = (here.astype(jnp.float32) == goal).astype(jnp.float32)
    covered = jnp.sum(picked, axis=-1, keepdims=True) > 0.5
    picked = picked.astype(jnp.bfloat16)
    chunk = 512

    def place(i, carry):
        cols = pl.ds(pl.multiple_of(i * chunk, chunk), chunk)
        rows_kv = kvbuf[:, :, cols].reshape(keys, chunk)
        new = jnp.dot(picked, rows_kv, preferred_element_type=jnp.float32)
        old = cachebuf[:, :, cols].reshape(slots_here * PAGE, chunk)
        both = jnp.where(covered, new, old.astype(jnp.float32)).astype(jnp.bfloat16)
        placedbuf[:, :, cols] = both.reshape(slots_here, PAGE, chunk)
        return carry

    lax.fori_loop(0, kv_in.shape[1] // chunk, place, 0)
    store_cache = pltpu.make_async_copy(placedbuf, cache_out, local_sem.at[8])
    store_cache.start()

    def forward_gate(slot):
        w_wait(slot, 0)
        w_copy(slot, 0, Q_NEXT).start()

    def forward_up(slot):
        w_wait(slot, 1)
        w_copy(slot, 1, Q_PREV).start()

    forward_gate(prev_row + lead)
    forward_gate(prev_row + 1 - lead)
    forward_up(next_row + lead)
    nrm_ring[1]()
    forward_up(next_row + 1 - lead)
    nrm_ring[2]()
    nrm_ring[3]()
    nrm_ring[4]()
    nrm_ring[5]()

    parts = 2
    per = N_TOK // parts

    def project(slot):
        qq = slot // 2
        pp = (slot % 2) * 2 + (c + qq) % 2
        column = pl.multiple_of(grp_of(pp, qq) * units + x_col, COLS)

        def tile(i, carry):
            tokens = normbuf[pl.ds(i * per, per)].reshape(per * rows, WIDTH)
            sums = jnp.dot(tokens, wbuf[slot], preferred_element_type=jnp.float32)
            gate, up = sums[:, :COLS], sums[:, COLS:]
            value = gate / (1.0 + jnp.exp(-gate)) * up
            hidbuf[slot, pl.ds(i * per, per)] = value.astype(jnp.bfloat16).reshape(
                per, rows, COLS
            )
            return carry

        lax.fori_loop(0, parts, tile, 0)
        keep = pltpu.make_async_copy(
            hidbuf.at[slot, t], hid_out.at[:, pl.ds(column, COLS)], local_sem.at[9]
        )
        keep.start()

        def send(d, carry):
            there = (t + d) % N_TOK
            pltpu.make_async_remote_copy(
                src_ref=hidbuf.at[slot, there],
                dst_ref=hid_out.at[:, pl.ds(column, COLS)],
                send_sem=hid_send,
                recv_sem=hid_recv,
                device_id=(g, there),
                device_id_type=MESH,
            ).start()
            return carry

        lax.fori_loop(1, N_TOK, send, 0)
        keep.wait()

    def own_row(i, carry):
        project(q * 2 + i)
        return carry

    lax.fori_loop(0, 2, own_row, 0)

    def near_rows(i, carry):
        slot = jnp.where(i % 2 == 0, prev_row, next_row) + jnp.where(
            i < 2, lead, 1 - lead
        )
        prev = i % 2 == 0

        @pl.when(prev)
        def _():
            w_wait(slot, 1)

        @pl.when(jnp.logical_not(prev))
        def _():
            w_wait(slot, 0)

        project(slot)
        return carry

    lax.fori_loop(0, 4, near_rows, 0)
    far_row = wrap(q + 2) * 2

    def far_rows(i, carry):
        slot = far_row + jnp.where(i == 0, lead, 1 - lead)
        w_wait(slot, 0)
        w_wait(slot, 1)
        project(slot)
        return carry

    lax.fori_loop(0, 2, far_rows, 0)

    store_att.wait()
    store_cache.wait()
    for d in range(1, N_TOK):
        pass
    pltpu.make_async_copy(
        segbuf.at[pl.ds(0, N_TOK - 1)], segbuf.at[pl.ds(0, N_TOK - 1)], seg_send
    ).wait()
    kv_ring[6]()
    nrm_ring[6]()

    @pl.when(source)
    def _():
        for m in range(2):
            for way in range(4):
                w_copy(own_slot, m, way).wait_send()
            w_copy(far_slot, m, Q_NEXT).wait_send()
            w_copy(far_slot, m, Q_PREV).wait_send()

    @pl.when(jnp.logical_not(source))
    def _():
        w_copy(prev_slot, 0, P_NEXT).wait_send()
        w_copy(next_slot, 1, P_PREV).wait_send()
        for m in range(2):
            for slot in (prev_slot, next_slot):
                w_copy(slot, m, Q_NEXT).wait_send()
                w_copy(slot, m, Q_PREV).wait_send()

    for i in range(2):
        w_copy(prev_row + i, 0, Q_NEXT).wait_send()
        w_copy(next_row + i, 1, Q_PREV).wait_send()

    whole = hidbuf.at[:, pl.ds(0, N_TOK - 1)]
    pltpu.make_async_copy(whole, whole, hid_send).wait()
    pltpu.make_async_copy(whole, whole, hid_recv).wait()


def on_device(
    queries,
    rotated_keys_values,
    prompt_window_index,
    residual,
    ffn_gain,
    gate_weight,
    up_weight,
    paged_cache,
    page_table,
):
    rows = queries.shape[0]
    kv_width = rotated_keys_values.shape[1]
    hidden_width = gate_weight.shape[1] * SIDE * SIDE
    any_space = pl.BlockSpec(memory_space=pl.ANY)
    vmem = pl.BlockSpec(memory_space=pltpu.VMEM)
    bf16 = jnp.bfloat16
    dma = pltpu.SemaphoreType.DMA
    outs = pl.pallas_call(
        kernel,
        out_shape=(
            jax.ShapeDtypeStruct(residual.shape, bf16),
            jax.ShapeDtypeStruct((rows, hidden_width), bf16),
            jax.ShapeDtypeStruct(paged_cache.shape, bf16),
        ),
        in_specs=[
            any_space,
            any_space,
            vmem,
            any_space,
            vmem,
            any_space,
            any_space,
            any_space,
            vmem,
        ],
        out_specs=(any_space, any_space, any_space),
        scratch_shapes=[
            pltpu.VMEM(queries.shape, bf16),
            pltpu.VMEM((N_TOK, rows, kv_width), bf16),
            pltpu.VMEM((N_TOK, 1, rows), jnp.int32),
            pltpu.VMEM(residual.shape, bf16),
            pltpu.VMEM(paged_cache.shape, bf16),
            pltpu.VMEM(paged_cache.shape, bf16),
            pltpu.VMEM(residual.shape, bf16),
            pltpu.VMEM((rows, N_TOK * rows), jnp.float32),
            pltpu.VMEM((N_TOK, rows, WIDTH), bf16),
            pltpu.VMEM((8, WIDTH, 2 * COLS), bf16),
            pltpu.VMEM((8, N_TOK, rows, COLS), bf16),
            dma((9,)),
            dma((9,)),
            dma((9,)),
            dma((9,)),
            dma((4, 16)),
            dma((16,)),
            dma(()),
            dma(()),
            dma(()),
            dma(()),
            dma((10,)),
        ],
        compiler_params=pltpu.CompilerParams(
            collective_id=0,
            has_side_effects=True,
            vmem_limit_bytes=63 * 1024 * 1024,
        ),
        name="layer",
    )(
        queries,
        rotated_keys_values,
        prompt_window_index,
        residual,
        ffn_gain.reshape(1, -1),
        gate_weight,
        up_weight,
        paged_cache,
        page_table,
    )
    return tuple(outs)


def solution(mesh):
    in_specs = (
        P(("grp", "tok"), None),
        P(("grp", "tok"), None),
        P("grp", "tok"),
        P(("grp", "tok"), None),
        P(),
        P(None, "grp"),
        P(None, "grp"),
        P(("grp", "tok"), None, None),
        P("grp", None),
    )
    out_specs = (P(("grp", "tok"), None), P(("grp", "tok"), None), P(("grp", "tok"), None, None))
    return jax.shard_map(
        on_device, mesh=mesh, in_specs=in_specs, out_specs=out_specs, check_vma=False
    )
```

time: 341 us -> 149 us (0.44)
  waiting for transfers between devices: 202 us -> 0 us
  Pallas kernels: 0 us -> 143 us
  matrix products: 52.4 us -> 0 us
  local copies, waits for them, and re-layouts: 42.8 us -> 5.54 us
  between operations: 13.9 us -> 0.65 us
  other arithmetic: 11.5 us -> 0 us
  blocking collectives: 10.9 us -> 0 us
  starting transfers between devices: 5.31 us -> 0 us
    all_gather x4 -> x0, waiting for transfers between devices: 195 us -> none  [the longest x1 65.1 us: on_device(): lax.all_gather(up_cols, 'grp', axis=1, tiled=True)]
    pallas_call x0 -> x1, Pallas kernels: none -> 143 us  [on_device(): pl.pallas_call(kernel, out_shape=(jax.ShapeDtypeStruct(residual.shape, bf...]
    dot_general x5 -> x0, matrix products: 52.4 us -> none  [the longest x1 17.3 us: on_device(): up_sum = jnp.dot(shards, up_all, preferred_element_type=jnp.float32)]
    all_gather x1 -> x0, blocking collectives: 10.9 us -> none  [on_device(): seg_piece = lax.all_gather(own_segment, 'tok', axis=0, tiled=True)]
    unnamed x22 -> x7, local copies, waits for them, and re-layouts: 15.2 us -> 5.54 us
    all_to_all x1 -> x0, waiting for transfers between devices: 7.58 us -> none  [on_device(): lax.all_to_all(produced, 'tok', split_axis=0, concat_axis=1, tiled=True)]
    reshape x1 -> x0, local copies, waits for them, and re-layouts: 7.45 us -> none  [on_device(): key_value_portion.reshape(page_count, PAGE_TOKENS * kv_width)]
    reduce_sum x2 -> x0, other arithmetic: 6.82 us -> none  [the longest x1 5.02 us: on_device(): run_sum = jnp.sum(weights, axis=-1)]
  transfers between devices with their start and end apart: 5 -> 0, of which waited for: 5 -> 0; matrix products, arithmetic and copies ran while one was open for 22% -> 0% of each run, Pallas kernels for 0% -> 0%
where the time goes in v1:
time: 149 us
  Pallas kernels  143 us (96%)
  local copies, waits for them, and re-layouts  5.54 us (4%)
    pallas_call x1, Pallas kernels, on_device(): pl.pallas_call(kernel, out_shape=(jax.ShapeDtypeStruct(residual.shape, bf...  143 us
    unnamed x7, local copies, waits for them, and re-layouts  5.54 us

profile of v1, /device:TPU:25, one launch (start us, length us, event | category | flops | bytes accessed | tf_op | source)
XLA Modules:
  0.0 149.1 jit_solution(11073608639252096509)
XLA Ops:
  0.6 142.9 %layer.1 = (bf16[128,5120]{1,0:T(8,128)(2,1)}, bf16[128,8192]{1,0:T(8,128)(2,1)}, bf16[16,16,2048]{2,1,0:T(8,128)(2,1)}) custom-call(bf16[128,5120]{1,0:T(8,128)(2,1)} %q_in.1, bf16[128,2048]{1,0:T(8,128)(2,1)} %kv_in.1, s32[1,128]{1,0:T(1,128)} %seg_in.1, bf16[128,5120]{1,0:T(8,128)(2,1)} %res_in.1, f32[1,5120]{1,0:T(1,128)} %bitcast.1, ...), custom_call_target="tpu_custom_call" | custom-call | tf_op jit(solution)/shard_map/layer/pallas_call | solution.py:521
  143.6 0.0 copy-start
  143.6 2.6 %copy.15 = bf16[128,5120]{1,0:T(8,128)(2,1)} copy(bf16[128,5120]{1,0:T(8,128)(2,1)} %get-tuple-element.6) | data formatting | bytes 2621440
  146.2 0.0 copy-done
  146.2 0.0 copy-start.1
  146.2 1.3 copy.16
  147.5 0.6 copy-done.1
  148.2 1.0 copy.17
Async XLA Ops:
  143.6 2.6 %copy-start = (bf16[128,8192]{1,0:T(8,128)(2,1)S(1)}, bf16[128,8192]{1,0:T(8,128)(2,1)}, u32[]{:S(2)}) copy-start(bf16[128,8192]{1,0:T(8,128)(2,1)} %get-tuple-element.7) | copy-start | bytes 6291460
  146.2 2.0 %copy-start.1 = (bf16[16,16,2048]{2,1,0:T(8,128)(2,1)S(1)}, bf16[16,16,2048]{2,1,0:T(8,128)(2,1)}, u32[]{:S(2)}) copy-start(bf16[16,16,2048]{2,1,0:T(8,128)(2,1)} %get-tuple-element.8) | copy-start | bytes 3145732

commit v2 on v1

--- a/solution.py
+++ b/solution.py
@@ -41,6 +41,8 @@
     placedbuf,
     attbuf,
     biasbuf,
+    statbuf,
+    scalebuf,
     normbuf,
     wbuf,
     hidbuf,
@@ -52,6 +54,8 @@
     w_recv,
     seg_send,
     seg_recv,
+    stat_send,
+    stat_recv,
     hid_send,
     hid_recv,
     local_sem,
@@ -65,74 +69,163 @@
     t = lax.axis_index("tok")
     x, c = t // 2, t % 2
     z, y = g // SIDE, g % SIDE
-    first = c == 0
-    p = jnp.where(first, z, y)
-    q = jnp.where(first, y, z)
-    p_step = jnp.where(first, SIDE, 1)
-    q_step = jnp.where(first, 1, SIDE)
-
     def wrap(v):
         return (v + SIDE) % SIDE
 
-    def grp_of(pp, qq):
-        return pp * p_step + qq * q_step
+    def grp_of(zz, yy):
+        return zz * SIDE + yy
 
     x_next = (g, wrap(x + 1) * 2 + c)
     x_prev = (g, wrap(x - 1) * 2 + c)
     sibling = (g, x * 2 + 1 - c)
-    p_next = (grp_of(wrap(p + 1), q), t)
-    p_prev = (grp_of(wrap(p - 1), q), t)
-    q_next = (grp_of(p, wrap(q + 1)), t)
-    q_prev = (grp_of(p, wrap(q - 1)), t)
-    plane = (p_next, p_prev, q_next, q_prev)
+    plane = (
+        grp_of(wrap(z + 1), y),
+        grp_of(wrap(z - 1), y),
+        grp_of(z, wrap(y + 1)),
+        grp_of(z, wrap(y - 1)),
+    )
     P_NEXT, P_PREV, Q_NEXT, Q_PREV = 0, 1, 2, 3
+
+    source = (z + y) % 2 == c
+    relay = jnp.logical_not(source)
+    x_col = pl.multiple_of(x * COLS, COLS)
+    deep = WIDTH // 2
+
+    class Walk:
+        def __init__(self, m):
+            self.m = m
+            self.z_first = c == m
+            self.p = jnp.where(self.z_first, z, y)
+            self.q = jnp.where(self.z_first, y, z)
+            z_ways, y_ways = plane[:2], plane[2:]
+            self.ways = [
+                (jnp.where(self.z_first, a, b), t)
+                for a, b in zip(z_ways + y_ways, y_ways + z_ways)
+            ]
+
+        def slot(self, dp, dq):
+            pp, qq = wrap(self.p + dp), wrap(self.q + dq)
+            zz = jnp.where(self.z_first, pp, qq)
+            yy = jnp.where(self.z_first, qq, pp)
+            return yy * 2 + zz // 2
+
+        def own(self, h):
+            ref = (gate_in, up_in)[self.m]
+            return ref.at[pl.ds(h * deep, deep), pl.ds(x_col, COLS)]
+
+        def piece(self, slot, h):
+            return wbuf.at[slot, self.m, pl.ds(h * deep, deep)]
+
+        def copy(self, slot, h, way, src=None):
+            return pltpu.make_async_remote_copy(
+                src_ref=self.piece(slot, h) if src is None else src,
+                dst_ref=self.piece(slot, h),
+                send_sem=w_send.at[self.m, way, slot * 2 + h],
+                recv_sem=w_recv.at[self.m, slot * 2 + h],
+                device_id=self.ways[way],
+                device_id_type=MESH,
+            )
+
+        def wait(self, slot, h):
+            self.copy(slot, h, 0).wait_recv()
+
+        def pass_on(self, dp, dq, h, *ways):
+            slot = self.slot(dp, dq)
+            self.wait(slot, h)
+            for way in ways:
+                self.copy(slot, h, way).start()
+
+    walks = (Walk(0), Walk(1))
+    own_slot = walks[0].slot(0, 0)
+
+    load_own = [
+        pltpu.make_async_copy(
+            w.own(h), w.piece(own_slot, h), local_sem.at[9 + 2 * w.m + h]
+        )
+        for h in range(2)
+        for w in walks
+    ]
+
+    @pl.when(source)
+    def _():
+        for load in load_own:
+            load.start()
 
     barrier = pltpu.get_barrier_semaphore()
     for there in plane:
-        pl.semaphore_signal(barrier, inc=1, device_id=there, device_id_type=MESH)
+        pl.semaphore_signal(
+            barrier, inc=1, device_id=(there, t), device_id_type=MESH
+        )
     for d in range(1, N_TOK):
         pl.semaphore_signal(
             barrier, inc=1, device_id=(g, (t + d) % N_TOK), device_id_type=MESH
         )
     pl.semaphore_wait(barrier, N_TOK + 3)
 
-    source = (p + q) % 2 == c
-    x_col = pl.multiple_of(x * COLS, COLS)
-    own_slot = q * 2 + p // 2
-    far_slot = q * 2 + 1 - p // 2
-    prev_slot = q * 2 + wrap(p - 1) // 2
-    next_slot = q * 2 + wrap(p + 1) // 2
-
-    def piece(slot, m):
-        return wbuf.at[slot, :, pl.ds(m * COLS, COLS)]
-
-    def own_piece(m):
-        return (gate_in, up_in)[m].at[:, pl.ds(x_col, COLS)]
-
-    def w_copy(slot, m, way, src=None):
-        return pltpu.make_async_remote_copy(
-            src_ref=piece(slot, m) if src is None else src,
-            dst_ref=piece(slot, m),
-            send_sem=w_send.at[way, slot * 2 + m],
-            recv_sem=w_recv.at[slot * 2 + m],
-            device_id=plane[way],
-            device_id_type=MESH,
-        )
-
-    def w_wait(slot, m):
-        w_copy(slot, m, 0).wait_recv()
-
     @pl.when(source)
     def _():
-        for m in range(2):
+        for i in range(4):
+            load_own[i].wait()
             for way in range(4):
-                w_copy(own_slot, m, way, own_piece(m)).start()
-
-    def ring(buf, send, recv):
+                walks[i % 2].copy(own_slot, i // 2, way).start()
+
+    def near_first():
+        @pl.when(relay)
+        def _():
+            for w in walks:
+                w.pass_on(-1, 0, 0, P_NEXT, Q_NEXT, Q_PREV)
+                w.pass_on(1, 0, 0, Q_NEXT, Q_PREV)
+            for w in walks:
+                w.pass_on(0, -1, 0, Q_NEXT)
+
+    def near_second():
+        @pl.when(relay)
+        def _():
+            for w in walks:
+                w.pass_on(1, 0, 1, P_PREV, Q_NEXT, Q_PREV)
+                w.pass_on(-1, 0, 1, Q_NEXT, Q_PREV)
+            for w in walks:
+                w.pass_on(0, 1, 1, Q_PREV)
+
+    def far_half(h):
+        @pl.when(source)
+        def _():
+            for w in walks:
+                w.pass_on(2, 0, h, Q_NEXT, Q_PREV)
+
+    def rows_first():
+        for w in walks:
+            @pl.when(source)
+            def _(w=w):
+                w.pass_on(-1, -1, 0, Q_NEXT)
+                w.pass_on(1, -1, 0, Q_NEXT)
+
+    def rows_far_first():
+        for w in walks:
+            @pl.when(relay)
+            def _(w=w):
+                w.pass_on(2, -1, 0, Q_NEXT)
+
+    def rows_second():
+        for w in walks:
+            @pl.when(source)
+            def _(w=w):
+                w.pass_on(-1, 1, 1, Q_PREV)
+                w.pass_on(1, 1, 1, Q_PREV)
+
+    def rows_far_second():
+        for w in walks:
+            @pl.when(relay)
+            def _(w=w):
+                w.pass_on(2, 1, 1, Q_PREV)
+
+    def ring(buf, send, recv, cols=None):
         def copy(slot, n_send, n_recv, there, part=None, src=None):
             ref = buf.at[slot]
             if part is not None:
                 ref = ref.at[pl.ds(part * half, half)]
+            if cols is not None:
+                ref = ref.at[:, pl.ds(*cols)]
             return pltpu.make_async_remote_copy(
                 src_ref=ref if src is None else src,
                 dst_ref=ref,
@@ -219,18 +312,11 @@
     load_res = pltpu.make_async_copy(res_in, resbuf, local_sem.at[2])
     load_cache = pltpu.make_async_copy(cache_in, cachebuf, local_sem.at[3])
     load_seg = pltpu.make_async_copy(seg_in, segbuf.at[t], local_sem.at[4])
-    load_gate = pltpu.make_async_copy(own_piece(0), piece(own_slot, 0), local_sem.at[5])
-    load_up = pltpu.make_async_copy(own_piece(1), piece(own_slot, 1), local_sem.at[6])
     load_kv.start()
     load_q.start()
     load_seg.start()
     load_res.start()
     load_cache.start()
-
-    @pl.when(source)
-    def _():
-        load_gate.start()
-        load_up.start()
 
     load_seg.wait()
     pltpu.make_async_copy(segbuf.at[pl.ds(0, N_TOK - 1)], segbuf.at[pl.ds(0, N_TOK - 1)], seg_recv).wait()
@@ -243,16 +329,7 @@
 
     kv_ring[1]()
 
-    @pl.when(jnp.logical_not(source))
-    def _():
-        w_wait(prev_slot, 0)
-        w_copy(prev_slot, 0, P_NEXT).start()
-        w_copy(prev_slot, 0, Q_NEXT).start()
-        w_copy(prev_slot, 0, Q_PREV).start()
-        w_wait(next_slot, 0)
-        w_copy(next_slot, 0, Q_NEXT).start()
-        w_copy(next_slot, 0, Q_PREV).start()
-
+    near_first()
     kv_ring[2]()
     load_kv.wait()
     load_q.wait()
@@ -287,57 +364,50 @@
             a = a.astype(jnp.bfloat16)
             attbuf[:, cols] = a
             a = a.astype(jnp.float32)
+            normbuf[t, :, cols] = (a * gain_in[:, cols]).astype(jnp.bfloat16)
             squares = squares + a * a
         return squares
 
-    squares = lax.fori_loop(
-        0, KV_HEADS // 2, attend, jnp.zeros((rows, HEAD), jnp.float32)
-    )
-
-    @pl.when(jnp.logical_not(source))
-    def _():
-        w_wait(prev_slot, 1)
-        w_copy(prev_slot, 1, Q_NEXT).start()
-        w_copy(prev_slot, 1, Q_PREV).start()
-        w_wait(next_slot, 1)
-        w_copy(next_slot, 1, P_PREV).start()
-        w_copy(next_slot, 1, Q_NEXT).start()
-        w_copy(next_slot, 1, Q_PREV).start()
-
-    @pl.when(source)
-    def _():
-        load_gate.wait()
-        load_up.wait()
-        w_wait(far_slot, 0)
-        w_copy(far_slot, 0, Q_NEXT).start()
-        w_copy(far_slot, 0, Q_PREV).start()
-
-    squares = lax.fori_loop(KV_HEADS // 2, KV_HEADS, attend, squares)
+    width = 2 * GROUP * HEAD
+    rings = [
+        ring(normbuf, nrm_send.at[i], nrm_recv.at[i], (i * width, width))
+        for i in range(KV_HEADS // 2)
+    ]
+    squares = jnp.zeros((rows, HEAD), jnp.float32)
+    squares = lax.fori_loop(0, 2, attend, squares)
+    rings[0][0]()
+    far_half(0)
+    squares = lax.fori_loop(2, 4, attend, squares)
+    rings[1][0]()
+    near_second()
+    squares = lax.fori_loop(4, 6, attend, squares)
+    rings[2][0]()
+    rings[0][1]()
+    squares = lax.fori_loop(6, 8, attend, squares)
+    rings[3][0]()
     mean = jnp.sum(squares, axis=-1, keepdims=True) * (1.0 / WIDTH)
-    inverse = lax.rsqrt(mean + 1e-6)
-
-    def norm(h, carry):
-        cols = pl.ds(pl.multiple_of(h * (GROUP * HEAD), HEAD), GROUP * HEAD)
-        a = attbuf[:, cols].astype(jnp.float32) * inverse * gain_in[:, cols]
-        normbuf[t, :, cols] = a.astype(jnp.bfloat16)
-        return carry
-
-    lax.fori_loop(0, KV_HEADS, norm, 0)
-
-    nrm_ring = ring(normbuf, nrm_send, nrm_recv)
-    nrm_ring[0]()
+    inverse = jnp.broadcast_to(lax.rsqrt(mean + 1e-6), (rows, rows))
+    scalebuf[t] = inverse
+    statbuf[t] = inverse.T[:1]
+
+    def stat_copy(d):
+        return pltpu.make_async_remote_copy(
+            src_ref=statbuf.at[t],
+            dst_ref=statbuf.at[t],
+            send_sem=stat_send,
+            recv_sem=stat_recv,
+            device_id=(g, (t + d) % N_TOK),
+            device_id_type=MESH,
+        )
+
+    for d in range(1, N_TOK):
+        stat_copy(d).start()
     store_att = pltpu.make_async_copy(attbuf, att_out, local_sem.at[7])
     store_att.start()
-
-    @pl.when(source)
-    def _():
-        w_wait(far_slot, 1)
-        w_copy(far_slot, 1, Q_NEXT).start()
-        w_copy(far_slot, 1, Q_PREV).start()
-
-    prev_row = wrap(q - 1) * 2
-    next_row = wrap(q + 1) * 2
-    lead = p // 2
+    far_half(1)
+    rings[0][2]()
+    rows_first()
+    rings[1][1]()
 
     load_cache.wait()
     table = jnp.broadcast_to(table_in[...], (8, table_in.shape[1]))
@@ -372,47 +442,78 @@
     store_cache = pltpu.make_async_copy(placedbuf, cache_out, local_sem.at[8])
     store_cache.start()
 
-    def forward_gate(slot):
-        w_wait(slot, 0)
-        w_copy(slot, 0, Q_NEXT).start()
-
-    def forward_up(slot):
-        w_wait(slot, 1)
-        w_copy(slot, 1, Q_PREV).start()
-
-    forward_gate(prev_row + lead)
-    forward_gate(prev_row + 1 - lead)
-    forward_up(next_row + lead)
-    nrm_ring[1]()
-    forward_up(next_row + 1 - lead)
-    nrm_ring[2]()
-    nrm_ring[3]()
-    nrm_ring[4]()
-    nrm_ring[5]()
+    rows_far_first()
+    rings[1][2]()
+    rings[2][1]()
+    rows_second()
+    rings[2][2]()
+    rings[3][1]()
+    some = statbuf.at[pl.ds(0, N_TOK - 1)]
+    pltpu.make_async_copy(some, some, stat_recv).wait()
+
+    def spread_scale(d, carry):
+        there = (t + d) % N_TOK
+        scalebuf[there] = jnp.broadcast_to(statbuf[there], (rows, rows)).T
+        return carry
+
+    lax.fori_loop(1, N_TOK, spread_scale, 0)
+    rows_far_second()
+    rings[3][2]()
+    for part in rings:
+        part[3]()
+        part[4]()
+        part[5]()
 
     parts = 2
     per = N_TOK // parts
 
-    def project(slot):
-        qq = slot // 2
-        pp = (slot % 2) * 2 + (c + qq) % 2
-        column = pl.multiple_of(grp_of(pp, qq) * units + x_col, COLS)
-
-        def tile(i, carry):
-            tokens = normbuf[pl.ds(i * per, per)].reshape(per * rows, WIDTH)
-            sums = jnp.dot(tokens, wbuf[slot], preferred_element_type=jnp.float32)
-            gate, up = sums[:, :COLS], sums[:, COLS:]
+    def choose(i, values):
+        out = jnp.int32(values[-1])
+        for k in range(len(values) - 1):
+            out = jnp.where(i == k, values[k], out)
+        return out
+
+    def project(i, carry):
+        dz = jnp.where(
+            source,
+            choose(i, (0, 2, 0, 1, 1, 3, 3, 2)),
+            choose(i, (1, 3, 0, 0, 3, 2, 1, 2)),
+        )
+        dy = jnp.where(
+            source,
+            choose(i, (0, 0, 2, 1, 3, 1, 3, 2)),
+            choose(i, (0, 0, 1, 3, 2, 3, 2, 1)),
+        )
+        zz, yy = wrap(z + dz), wrap(y + dy)
+        slot = yy * 2 + zz // 2
+        for w in walks:
+            dq = jnp.where(w.z_first, dy, dz)
+
+            @pl.when((dq == 1) | (dq == 2))
+            def _(w=w):
+                w.wait(slot, 0)
+
+            @pl.when((dq == 3) | (dq == 2))
+            def _(w=w):
+                w.wait(slot, 1)
+
+        column = pl.multiple_of(grp_of(zz, yy) * units + x_col, COLS)
+
+        def tile(k, carry):
+            some = pl.ds(k * per, per)
+            tokens = normbuf[some].reshape(per * rows, WIDTH)
+            both = jnp.concatenate([wbuf[slot, 0], wbuf[slot, 1]], axis=1)
+            sums = jnp.dot(tokens, both, preferred_element_type=jnp.float32)
+            scale = scalebuf[some].reshape(per * rows, COLS)
+            gate, up = sums[:, :COLS] * scale, sums[:, COLS:] * scale
             value = gate / (1.0 + jnp.exp(-gate)) * up
-            hidbuf[slot, pl.ds(i * per, per)] = value.astype(jnp.bfloat16).reshape(
-                per, rows, COLS
-            )
+            hidbuf[slot, some] = value.astype(jnp.bfloat16).reshape(per, rows, COLS)
             return carry
 
         lax.fori_loop(0, parts, tile, 0)
-        keep = pltpu.make_async_copy(
-            hidbuf.at[slot, t], hid_out.at[:, pl.ds(column, COLS)], local_sem.at[9]
-        )
-        keep.start()
+        pltpu.make_async_copy(
+            hidbuf.at[slot, t], hid_out.at[:, pl.ds(column, COLS)], hid_recv
+        ).start()
 
         def send(d, carry):
             there = (t + d) % N_TOK
@@ -427,77 +528,48 @@
             return carry
 
         lax.fori_loop(1, N_TOK, send, 0)
-        keep.wait()
-
-    def own_row(i, carry):
-        project(q * 2 + i)
         return carry
 
-    lax.fori_loop(0, 2, own_row, 0)
-
-    def near_rows(i, carry):
-        slot = jnp.where(i % 2 == 0, prev_row, next_row) + jnp.where(
-            i < 2, lead, 1 - lead
-        )
-        prev = i % 2 == 0
-
-        @pl.when(prev)
-        def _():
-            w_wait(slot, 1)
-
-        @pl.when(jnp.logical_not(prev))
-        def _():
-            w_wait(slot, 0)
-
-        project(slot)
-        return carry
-
-    lax.fori_loop(0, 4, near_rows, 0)
-    far_row = wrap(q + 2) * 2
-
-    def far_rows(i, carry):
-        slot = far_row + jnp.where(i == 0, lead, 1 - lead)
-        w_wait(slot, 0)
-        w_wait(slot, 1)
-        project(slot)
-        return carry
-
-    lax.fori_loop(0, 2, far_rows, 0)
+    lax.fori_loop(0, 8, project, 0)
 
     store_att.wait()
     store_cache.wait()
-    for d in range(1, N_TOK):
-        pass
     pltpu.make_async_copy(
         segbuf.at[pl.ds(0, N_TOK - 1)], segbuf.at[pl.ds(0, N_TOK - 1)], seg_send
     ).wait()
     kv_ring[6]()
-    nrm_ring[6]()
+    pltpu.make_async_copy(some, some, stat_send).wait()
+    for part in rings:
+        part[6]()
 
     @pl.when(source)
     def _():
-        for m in range(2):
-            for way in range(4):
-                w_copy(own_slot, m, way).wait_send()
-            w_copy(far_slot, m, Q_NEXT).wait_send()
-            w_copy(far_slot, m, Q_PREV).wait_send()
-
-    @pl.when(jnp.logical_not(source))
+        for w in walks:
+            for h in range(2):
+                for way in range(4):
+                    w.copy(own_slot, h, way).wait_send()
+                w.copy(w.slot(2, 0), h, Q_NEXT).wait_send()
+                w.copy(w.slot(2, 0), h, Q_PREV).wait_send()
+            for dp in (-1, 1):
+                w.copy(w.slot(dp, -1), 0, Q_NEXT).wait_send()
+                w.copy(w.slot(dp, 1), 1, Q_PREV).wait_send()
+
+    @pl.when(relay)
     def _():
-        w_copy(prev_slot, 0, P_NEXT).wait_send()
-        w_copy(next_slot, 1, P_PREV).wait_send()
-        for m in range(2):
-            for slot in (prev_slot, next_slot):
-                w_copy(slot, m, Q_NEXT).wait_send()
-                w_copy(slot, m, Q_PREV).wait_send()
-
-    for i in range(2):
-        w_copy(prev_row + i, 0, Q_NEXT).wait_send()
-        w_copy(next_row + i, 1, Q_PREV).wait_send()
+        for w in walks:
+            w.copy(w.slot(-1, 0), 0, P_NEXT).wait_send()
+            w.copy(w.slot(1, 0), 1, P_PREV).wait_send()
+            for h in range(2):
+                for dp in (-1, 1):
+                    w.copy(w.slot(dp, 0), h, Q_NEXT).wait_send()
+                    w.copy(w.slot(dp, 0), h, Q_PREV).wait_send()
+            for dp in (0, 2):
+                w.copy(w.slot(dp, -1), 0, Q_NEXT).wait_send()
+                w.copy(w.slot(dp, 1), 1, Q_PREV).wait_send()
 
     whole = hidbuf.at[:, pl.ds(0, N_TOK - 1)]
     pltpu.make_async_copy(whole, whole, hid_send).wait()
-    pltpu.make_async_copy(whole, whole, hid_recv).wait()
+    pltpu.make_async_copy(hidbuf, hidbuf, hid_recv).wait()
 
 
 def on_device(
@@ -546,20 +618,24 @@
             pltpu.VMEM(paged_cache.shape, bf16),
             pltpu.VMEM(residual.shape, bf16),
             pltpu.VMEM((rows, N_TOK * rows), jnp.float32),
+            pltpu.VMEM((N_TOK, 1, rows), jnp.float32),
+            pltpu.VMEM((N_TOK, rows, COLS), jnp.float32),
             pltpu.VMEM((N_TOK, rows, WIDTH), bf16),
-            pltpu.VMEM((8, WIDTH, 2 * COLS), bf16),
+            pltpu.VMEM((8, 2, WIDTH, COLS), bf16),
             pltpu.VMEM((8, N_TOK, rows, COLS), bf16),
             dma((9,)),
             dma((9,)),
-            dma((9,)),
-            dma((9,)),
-            dma((4, 16)),
-            dma((16,)),
+            dma((KV_HEADS // 2, 9)),
+            dma((KV_HEADS // 2, 9)),
+            dma((2, 4, 16)),
+            dma((2, 16)),
             dma(()),
             dma(()),
             dma(()),
             dma(()),
-            dma((10,)),
+            dma(()),
+            dma(()),
+            dma((13,)),
         ],
         compiler_params=pltpu.CompilerParams(
             collective_id=0,

time: 149 us -> 136 us (0.913)
  Pallas kernels: 143 us -> 129 us
    pallas_call x1, Pallas kernels: 143 us -> 129 us  [on_device(): pl.pallas_call(kernel, out_shape=(jax.ShapeDtypeStruct(residual.shape, bf...]
where the time goes in v2:
time: 136 us; the launch traced here: 135 us
  Pallas kernels  129 us (95%)
  local copies, waits for them, and re-layouts  5.54 us (4%)
    pallas_call x1, Pallas kernels, on_device(): pl.pallas_call(kernel, out_shape=(jax.ShapeDtypeStruct(residual.shape, bf...  129 us
    unnamed x7, local copies, waits for them, and re-layouts  5.54 us

profile of v2, /device:TPU:25, one launch (start us, length us, event | category | flops | bytes accessed | tf_op | source)
XLA Modules:
  0.0 134.7 jit_solution(13192021539823875217)
XLA Ops:
  0.6 128.6 %layer.1 = (bf16[128,5120]{1,0:T(8,128)(2,1)}, bf16[128,8192]{1,0:T(8,128)(2,1)}, bf16[16,16,2048]{2,1,0:T(8,128)(2,1)}) custom-call(bf16[128,5120]{1,0:T(8,128)(2,1)} %q_in.1, bf16[128,2048]{1,0:T(8,128)(2,1)} %kv_in.1, s32[1,128]{1,0:T(1,128)} %seg_in.1, bf16[128,5120]{1,0:T(8,128)(2,1)} %res_in.1, f32[1,5120]{1,0:T(1,128)} %bitcast.1, ...), custom_call_target="tpu_custom_call" | custom-call | tf_op jit(solution)/shard_map/layer/pallas_call | solution.py:593
  129.2 0.0 copy-start
  129.2 2.6 %copy.15 = bf16[128,5120]{1,0:T(8,128)(2,1)} copy(bf16[128,5120]{1,0:T(8,128)(2,1)} %get-tuple-element.6) | data formatting | bytes 2621440
  131.8 0.0 copy-done
  131.8 0.0 copy-start.1
  131.8 1.3 copy.16
  133.1 0.6 copy-done.1
  133.8 1.0 copy.17
Async XLA Ops:
  129.2 2.6 %copy-start = (bf16[128,8192]{1,0:T(8,128)(2,1)S(1)}, bf16[128,8192]{1,0:T(8,128)(2,1)}, u32[]{:S(2)}) copy-start(bf16[128,8192]{1,0:T(8,128)(2,1)} %get-tuple-element.7) | copy-start | bytes 6291460
  131.8 2.0 %copy-start.1 = (bf16[16,16,2048]{2,1,0:T(8,128)(2,1)S(1)}, bf16[16,16,2048]{2,1,0:T(8,128)(2,1)}, u32[]{:S(2)}) copy-start(bf16[16,16,2048]{2,1,0:T(8,128)(2,1)} %get-tuple-element.8) | copy-start | bytes 3145732

commit v3 on v2

--- a/solution.py
+++ b/solution.py
@@ -38,8 +38,6 @@
     segbuf,
     resbuf,
     cachebuf,
-    placedbuf,
-    attbuf,
     biasbuf,
     statbuf,
     scalebuf,
@@ -362,7 +360,7 @@
             cols = pl.ds(base + j * HEAD, HEAD)
             a = resbuf[:, cols].astype(jnp.float32) + out[j].astype(jnp.float32)
             a = a.astype(jnp.bfloat16)
-            attbuf[:, cols] = a
+            att_out[:, cols] = a
             a = a.astype(jnp.float32)
             normbuf[t, :, cols] = (a * gain_in[:, cols]).astype(jnp.bfloat16)
             squares = squares + a * a
@@ -402,8 +400,6 @@
 
     for d in range(1, N_TOK):
         stat_copy(d).start()
-    store_att = pltpu.make_async_copy(attbuf, att_out, local_sem.at[7])
-    store_att.start()
     far_half(1)
     rings[0][2]()
     rows_first()
@@ -435,12 +431,10 @@
         new = jnp.dot(picked, rows_kv, preferred_element_type=jnp.float32)
         old = cachebuf[:, :, cols].reshape(slots_here * PAGE, chunk)
         both = jnp.where(covered, new, old.astype(jnp.float32)).astype(jnp.bfloat16)
-        placedbuf[:, :, cols] = both.reshape(slots_here, PAGE, chunk)
+        cache_out[:, :, cols] = both.reshape(slots_here, PAGE, chunk)
         return carry
 
     lax.fori_loop(0, kv_in.shape[1] // chunk, place, 0)
-    store_cache = pltpu.make_async_copy(placedbuf, cache_out, local_sem.at[8])
-    store_cache.start()
 
     rows_far_first()
     rings[1][2]()
@@ -532,8 +526,6 @@
 
     lax.fori_loop(0, 8, project, 0)
 
-    store_att.wait()
-    store_cache.wait()
     pltpu.make_async_copy(
         segbuf.at[pl.ds(0, N_TOK - 1)], segbuf.at[pl.ds(0, N_TOK - 1)], seg_send
     ).wait()
@@ -593,9 +585,9 @@
     outs = pl.pallas_call(
         kernel,
         out_shape=(
-            jax.ShapeDtypeStruct(residual.shape, bf16),
-            jax.ShapeDtypeStruct((rows, hidden_width), bf16),
-            jax.ShapeDtypeStruct(paged_cache.shape, bf16),
+            pltpu.VMEM(residual.shape, bf16),
+            pltpu.VMEM((rows, hidden_width), bf16),
+            pltpu.VMEM(paged_cache.shape, bf16),
         ),
         in_specs=[
             any_space,
@@ -608,15 +600,13 @@
             any_space,
             vmem,
         ],
-        out_specs=(any_space, any_space, any_space),
+        out_specs=(vmem, vmem, vmem),
         scratch_shapes=[
             pltpu.VMEM(queries.shape, bf16),
             pltpu.VMEM((N_TOK, rows, kv_width), bf16),
             pltpu.VMEM((N_TOK, 1, rows), jnp.int32),
             pltpu.VMEM(residual.shape, bf16),
             pltpu.VMEM(paged_cache.shape, bf16),
-            pltpu.VMEM(paged_cache.shape, bf16),
-            pltpu.VMEM(residual.shape, bf16),
             pltpu.VMEM((rows, N_TOK * rows), jnp.float32),
             pltpu.VMEM((N_TOK, 1, rows), jnp.float32),
             pltpu.VMEM((N_TOK, rows, COLS), jnp.float32),
@@ -640,7 +630,7 @@
         compiler_params=pltpu.CompilerParams(
             collective_id=0,
             has_side_effects=True,
-            vmem_limit_bytes=63 * 1024 * 1024,
+            vmem_limit_bytes=50 * 1024 * 1024,
         ),
         name="layer",
     )(

time: 136 us -> 134 us (0.985)
  local copies, waits for them, and re-layouts: 5.54 us -> 3.35 us
    unnamed x7 -> x3, local copies, waits for them, and re-layouts: 5.54 us -> 3.35 us
where the time goes in v3:
time: 134 us; the launch traced here: 133 us
  Pallas kernels  129 us (96%)
  local copies, waits for them, and re-layouts  3.35 us (2%)
    pallas_call x1, Pallas kernels, on_device(): pl.pallas_call(kernel, out_shape=(pltpu.VMEM(residual.shape, bf16), pltpu...  129 us
    unnamed x3, local copies, waits for them, and re-layouts  3.35 us

profile of v3, /device:TPU:25, one launch (start us, length us, event | category | flops | bytes accessed | tf_op | source)
XLA Modules:
  0.0 132.6 jit_solution(17238711057180713680)
XLA Ops:
  0.6 128.6 %layer.1 = (bf16[128,5120]{1,0:T(8,128)(2,1)S(1)}, bf16[128,8192]{1,0:T(8,128)(2,1)S(1)}, bf16[16,16,2048]{2,1,0:T(8,128)(2,1)S(1)}) custom-call(bf16[128,5120]{1,0:T(8,128)(2,1)} %q_in.1, bf16[128,2048]{1,0:T(8,128)(2,1)} %kv_in.1, s32[1,128]{1,0:T(1,128)} %seg_in.1, bf16[128,5120]{1,0:T(8,128)(2,1)} %res_in.1, f32[1,5120]{1,0:T(1,128)} %bitcast.1, ...), custom_call_target="tpu_custom_call" | custom-call | tf_op jit(solution)/shard_map/layer/pallas_call | solution.py:585
  129.2 1.1 copy.15
  130.3 1.0 copy.17
  131.2 1.3 copy.16

commit v4 on v3

--- a/solution.py
+++ b/solution.py
@@ -458,7 +458,7 @@
         part[4]()
         part[5]()
 
-    parts = 2
+    parts = 1
     per = N_TOK // parts
 
     def choose(i, values):

time: 134 us -> 133 us (level)
  Pallas kernels: 129 us -> 127 us
    pallas_call x1, Pallas kernels: 129 us -> 127 us  [on_device(): pl.pallas_call(kernel, out_shape=(pltpu.VMEM(residual.shape, bf16), pltpu...]
where the time goes in v4:
time: 133 us; the launch traced here: 131 us
  Pallas kernels  127 us (95%)
  local copies, waits for them, and re-layouts  3.35 us (3%)
    pallas_call x1, Pallas kernels, on_device(): pl.pallas_call(kernel, out_shape=(pltpu.VMEM(residual.shape, bf16), pltpu...  127 us
    unnamed x3, local copies, waits for them, and re-layouts  3.35 us

profile of v4, /device:TPU:25, one launch (start us, length us, event | category | flops | bytes accessed | tf_op | source)
XLA Modules:
  0.0 131.0 jit_solution(11562444517536414479)
XLA Ops:
  0.6 127.0 %layer.1 = (bf16[128,5120]{1,0:T(8,128)(2,1)S(1)}, bf16[128,8192]{1,0:T(8,128)(2,1)S(1)}, bf16[16,16,2048]{2,1,0:T(8,128)(2,1)S(1)}) custom-call(bf16[128,5120]{1,0:T(8,128)(2,1)} %q_in.1, bf16[128,2048]{1,0:T(8,128)(2,1)} %kv_in.1, s32[1,128]{1,0:T(1,128)} %seg_in.1, bf16[128,5120]{1,0:T(8,128)(2,1)} %res_in.1, f32[1,5120]{1,0:T(1,128)} %bitcast.1, ...), custom_call_target="tpu_custom_call" | custom-call | tf_op jit(solution)/shard_map/layer/pallas_call | solution.py:585
  127.7 1.1 copy.15
  128.7 1.0 copy.17
  129.7 1.3 %copy.16 = bf16[128,8192]{1,0:T(8,128)(2,1)} copy(bf16[128,8192]{1,0:T(8,128)(2,1)S(1)} %get-tuple-element.4) | data formatting | bytes 4194304
